TPU v7x, 256 devices: a whole 4x4x8 slice. The times are simulated.
256 devices in a mesh: grp: 16 (over z, core), clu: 16 (over y, x).
Axes of the slice: x: 4, y: 4, z: 8, core: 2. Of those that a mesh axis runs over, the one named last changes fastest.
Arguments:
- strengths: bfloat16 [32768, 128], P(('grp', 'clu')), may hold values from -6 to 6
- adjoint_weights: bfloat16 [32768, 128], P(('grp', 'clu')), may hold values from -6 to 6
- kernels: bfloat16 [49152, 2, 128, 128], P(('grp', 'clu')), may hold values from -0.02734375 to 0.02734375
- target_ids: int32 [49152], P(('grp', 'clu')), may hold values from 0 to 255, as said below
- source_ids: int32 [49152], P(('grp', 'clu')), may hold values from 0 to 255, as said below
- live_slots: int32 [256], P(('grp', 'clu')), may hold values from 48 to 192, as said below
Outputs:
- potential: float32 [32768, 128], P(('grp', 'clu'))
- adjoint_field: float32 [32768, 128], P(('grp', 'clu'))
Inputs may be any that keep to these rules, and one draw needn't show every extreme that they name: `target_ids`: a slot's target block is one of the 16 blocks owned by the devices with the slot's grp index. `source_ids`: a slot's source block is owned by a device whose grp index equals that of the slot's device or differs from it by one. `live_slots`: some device uses all 192 slots.
All inputs are finite; a program needn't handle non-finite values.
Results may differ from a plain program's by a relative error of at most 0.0003.
Values may be sent and summed in bfloat16 or wider, within the bound.
A program may use at most 128 MiB of HBM per device.

v0:
```python
import jax
import jax.numpy as jnp
from jax import lax
from jax.sharding import PartitionSpec as P


def with_halo(cells, sides, width):
    for axis, dim in sides:
        count = lax.axis_size(axis)
        ends = count - 1
        head = lax.slice_in_dim(cells, 0, width, axis=dim)
        tail = lax.slice_in_dim(cells, cells.shape[dim] - width, cells.shape[dim], axis=dim)
        cells = jnp.concatenate(
            [
                lax.ppermute(tail, axis, [(i, (i + 1) % count) for i in range(ends)]),
                cells,
                lax.ppermute(head, axis, [((i + 1) % count, i) for i in range(ends)]),
            ],
            axis=dim,
        )
    return cells


def shifted(value, axis, steps):
    count = lax.axis_size(axis)
    first, last = (max(0, -steps), min(count, count - steps))
    return lax.ppermute(value, axis, [(source, source + steps) for source in range(first, last)])


def complex_join(prod, half):
    real_part = prod[:, 0, :, :half] - prod[:, 1, :, half:]
    imag_part = prod[:, 0, :, half:] + prod[:, 1, :, :half]
    return jnp.concatenate([real_part, imag_part], axis=-1)


def local(strengths, adjoint_weights, kernels, target_ids, source_ids, live_slots):
    panels = kernels.shape[2]
    width = strengths.shape[1]
    half = width // 2
    blocks = strengths.shape[0] // panels
    slots = kernels.shape[0]
    group_index = lax.axis_index("grp")
    group_blocks = lax.axis_size("clu") * blocks
    live = (jnp.arange(slots, dtype=jnp.int32) < live_slots[0]).astype(jnp.float32)
    local_target = target_ids - group_index * group_blocks
    offset = source_ids // group_blocks - group_index + 1
    within = source_ids % group_blocks
    rims = with_halo(strengths, (("grp", 0),), blocks * panels)
    widened, group_mu = (
        lax.all_gather(rims, "clu", axis=0, tiled=True),
        lax.all_gather(adjoint_weights, "clu", axis=0, tiled=True),
    )
    source_index = within // blocks * (3 * blocks) + offset * blocks + within % blocks
    picked = jnp.take(widened.reshape(-1, panels, width), source_index, axis=0)
    forward = jnp.einsum("nkpq,nqc->nkpc", kernels, picked, preferred_element_type=jnp.float32)
    forward = complex_join(forward, half).reshape(slots, panels * width)
    weights_out = jnp.take(group_mu.reshape(group_blocks, panels, width), local_target, axis=0)
    backward = jnp.einsum(
        "nkpq,npc->nkqc", kernels, weights_out, preferred_element_type=jnp.float32
    )
    backward = complex_join(backward, half).reshape(slots, panels * width)
    target_table = (
        local_target[None, :] == jnp.arange(group_blocks, dtype=jnp.int32)[:, None]
    ).astype(jnp.float32) * live[None, :]
    chosen = target_table
    potential = lax.psum_scatter(
        jnp.dot(
            chosen, forward, precision=lax.Precision.HIGHEST, preferred_element_type=jnp.float32
        ),
        "clu",
        scatter_dimension=0,
        tiled=True,
    )
    row_match = (within[None, :] == jnp.arange(group_blocks, dtype=jnp.int32)[:, None]).astype(
        jnp.float32
    )
    side_match = (offset[None, :] == jnp.arange(3, dtype=jnp.int32)[:, None]).astype(
        jnp.float32
    ) * live[None, :]
    source_table = row_match[:, None, :] * side_match[None, :, :]
    chosen = source_table
    shares = lax.psum_scatter(
        jnp.einsum(
            "ron,nx->rox",
            chosen,
            backward,
            precision=lax.Precision.HIGHEST,
            preferred_element_type=jnp.float32,
        ),
        "clu",
        scatter_dimension=0,
        tiled=True,
    )
    from_upper = shifted(shares[:, 0], "grp", -1)
    from_lower = shifted(shares[:, 2], "grp", 1)
    adjoint = shares[:, 1] + from_upper + from_lower
    return (potential.reshape(blocks * panels, width), adjoint.reshape(blocks * panels, width))


def solution(mesh):
    return jax.shard_map(
        local,
        mesh=mesh,
        in_specs=(
            P(("grp", "clu"), None),
            P(("grp", "clu"), None),
            P(("grp", "clu"), None, None, None),
            P(("grp", "clu")),
            P(("grp", "clu")),
            P(("grp", "clu")),
        ),
        out_specs=(P(("grp", "clu"), None), P(("grp", "clu"), None)),
        check_vma=False,
    )
```

profile of v0, /device:TPU:96, one launch (start us, length us, event | category | flops | bytes accessed | tf_op | source)
XLA Modules:
  0.0 351.1 jit_solution(8102390088822993544)
XLA Ops:
  7.2 0.0 all-gather.2.cloned.1.call-start
  7.2 1.9 collective-permute-start
  9.1 3.6 %collective-permute-start.1 = (bf16[128,128]{1,0:T(8,128)(2,1)}, bf16[128,128]{1,0:T(8,128)(2,1)S(1)}, u32[]{:S(2)}, u32[]{:S(2)}) collective-permute-start(bf16[128,128]{1,0:T(8,128)(2,1)} %param.6), channel_id=1, source_target_pairs={{16,0},{32,16},{48,32},{64,48},{80,64},{96,80},{112,96},{128,112},... | collective-permute-start | bytes 98312 | tf_op jit(solution)/shard_map/ppermute | solution.py:17
  12.8 0.7 compare_and_fusion
  13.5 24.5 %all_gather.7 = bf16[2048,128]{1,0:T(8,128)(2,1)S(1)} all-gather(bf16[128,128]{1,0:T(8,128)(2,1)} %param.7), channel_id=1, replica_groups=mesh['grp'=16,'clu'=16] {'clu'}, dimensions={0}, use_global_device_ids=true | all-gather | bytes 557056 | tf_op jit(solution)/shard_map/all_gather | solution.py:51
  38.0 8.1 %gather_fusion.1 = bf16[192,128,128]{2,1,0:T(8,128)(2,1)} fusion(bf16[16,128,128]{2,1,0:T(8,128)(2,1)S(1)} %bitcast.66, s32[1024]{0:T(1024)S(1)} %pad_clamp_fusion), kind=kCustom, calls=%fused_computation.1 | custom fusion | bytes 12583680 | tf_op jit(solution)/shard_map/jit(_take)/gather | solution.py:57
  46.1 0.0 copy-start
  46.1 14.2 %convolution_bitcast_fusion = f32[192,2,128,128]{2,3,1,0:T(8,128)} fusion(bf16[192,2,128,128]{3,2,1,0:T(8,128)(2,1)} %param.8, bf16[192,128,128]{2,1,0:T(8,128)(2,1)} %gather_fusion.1, pred[192]{0:T(512)(128)(4,1)S(1)} %get-tuple-element.4), kind=kOutput, calls=%fused_computation.7 | convolution fusion | flops 1613758464 | bytes 44040384 | tf_op jit(solution)/shard_map/nkpq,npc->nkqc/dot_general | solution.py:58
  60.9 0.0 collective-permute-done
  60.9 0.0 collective-permute-done.1
  61.0 0.0 copy-done
  61.0 0.6 pad_maximum_fusion.2
  61.6 0.0 all-gather.2.cloned.1.call-update
  61.6 0.0 all-reduce.5.cloned.1.call-start
  61.7 9.5 %fusion.3 = f32[192,128,64]{1,2,0:T(8,128)} fusion(f32[192,2,128,128]{2,3,1,0:T(8,128)} %convolution_bitcast_fusion), kind=kLoop, calls=%fused_computation.10 | loop fusion | flops 1572864 | bytes 18874368 | tf_op jit(solution)/shard_map/add | solution.py:32
  71.2 9.6 %fusion.5 = f32[192,128,64]{1,2,0:T(8,128)} fusion(f32[192,2,128,128]{2,3,1,0:T(8,128)} %convolution_bitcast_fusion), kind=kLoop, calls=%fused_computation.13 | loop fusion | flops 1572864 | bytes 18874368 | tf_op jit(solution)/shard_map/sub | solution.py:31
  80.8 11.3 %pad_maximum_fusion.1 = f32[192,128,128]{1,2,0:T(8,128)} fusion(f32[192,128,64]{1,2,0:T(8,128)} %fusion.3, f32[192,128,64]{1,2,0:T(8,128)} %fusion.5), kind=kLoop, calls=%fused_computation.6 | loop fusion | flops 3145728 | bytes 25165824 | tf_op jit(solution)/shard_map/concatenate | solution.py:33
  92.1 12.6 %copy.27 = f32[192,128,128]{2,1,0:T(8,128)} copy(f32[192,128,128]{1,2,0:T(8,128)} %pad_maximum_fusion.1) | data formatting | bytes 25165824 | tf_op jit(solution)/shard_map/concatenate | solution.py:33
  104.8 0.0 copy-start.1
  104.8 13.8 %reshape.122 = f32[192,16384,1]{1,0,2:T(8,128)} reshape(f32[192,128,128]{2,1,0:T(8,128)} %copy.27) | data formatting | bytes 25165824 | tf_op jit(solution)/shard_map/reshape | solution.py:61
  118.6 0.0 copy-done.1
  118.7 11.8 %fusion.19 = f32[16,3,16384]{2,0,1:T(8,128)} fusion(f32[192,16384,1]{1,0,2:T(8,128)} %reshape.122, f32[3,192]{1,0:T(4,128)S(1)} %fusion.28, f32[16,192]{1,0:T(8,128)S(1)} %fusion.24), kind=kOutput, calls=%fused_computation.35 | convolution fusion | flops 1811948544 | bytes 15743232 | tf_op jit(solution)/shard_map/ron,nx->rox/dot_general | solution.py:83
  130.5 0.0 all-gather.2.cloned.1.call-done
  130.5 9.5 %gather_fusion = bf16[192,128,128]{2,1,0:T(8,128)(2,1)} fusion(bf16[48,128,128]{2,1,0:T(8,128)(2,1)} %bitcast.68, s32[1024]{0:T(1024)S(1)} %pad_clamp_fusion.1), kind=kCustom, calls=%fused_computation | custom fusion | bytes 12583680 | tf_op jit(solution)/shard_map/jit(_take)/gather | solution.py:54
  140.0 16.4 %convolution_bitcast_fusion.1 = f32[192,2,128,128]{2,3,1,0:T(8,128)} fusion(bf16[192,2,128,128]{3,2,1,0:T(8,128)(2,1)} %param.8, bf16[192,128,128]{2,1,0:T(8,128)(2,1)} %gather_fusion, pred[192]{0:T(512)(128)(4,1)S(1)} %get-tuple-element.6), kind=kOutput, calls=%fused_computation.8 | convolution fusion | flops 1613758464 | bytes 44040384 | tf_op jit(solution)/shard_map/nkpq,nqc->nkpc/dot_general | solution.py:55
  156.4 9.5 %fusion.6 = f32[192,128,64]{1,2,0:T(8,128)} fusion(f32[192,2,128,128]{2,3,1,0:T(8,128)} %convolution_bitcast_fusion.1), kind=kLoop, calls=%fused_computation.16 | loop fusion | flops 1572864 | bytes 18874368 | tf_op jit(solution)/shard_map/add | solution.py:32
  165.9 9.5 %fusion.8 = f32[192,128,64]{1,2,0:T(8,128)} fusion(f32[192,2,128,128]{2,3,1,0:T(8,128)} %convolution_bitcast_fusion.1), kind=kLoop, calls=%fused_computation.19 | loop fusion | flops 1572864 | bytes 18874368 | tf_op jit(solution)/shard_map/sub | solution.py:31
  175.4 11.3 %pad_maximum_fusion = f32[192,128,128]{1,2,0:T(8,128)} fusion(f32[192,128,64]{1,2,0:T(8,128)} %fusion.6, f32[192,128,64]{1,2,0:T(8,128)} %fusion.8), kind=kLoop, calls=%fused_computation.5 | loop fusion | flops 3145728 | bytes 25165824 | tf_op jit(solution)/shard_map/concatenate | solution.py:33
  186.8 12.6 %copy.23 = f32[192,128,128]{2,1,0:T(8,128)} copy(f32[192,128,128]{1,2,0:T(8,128)} %pad_maximum_fusion) | data formatting | bytes 25165824 | tf_op jit(solution)/shard_map/concatenate | solution.py:33
  199.4 0.0 copy-start.2
  199.4 18.6 %fusion = f32[16,16384]{1,0:T(8,128)} fusion(f32[24,8,128,128]{3,2,1,0:T(8,128)} %bitcast.67, f32[192]{0:T(256)S(1)} %compare_convert_fusion, s32[192]{0:T(256)S(1)} %get-tuple-element.5), kind=kOutput, calls=%fused_computation.2 | convolution fusion | flops 603985920 | bytes 13633024 | tf_op jit(solution)/shard_map/dot_general | solution.py:67
  218.0 0.0 all-reduce.5.cloned.1.call-update
  218.0 0.0 copy-done.2
  218.0 0.6 dynamic-slice
  218.6 114.0 %all-reduce.5.cloned.1.call-done = (f32[16,16384]{1,0:T(8,128)}, f32[16,3,16384]{2,0,1:T(8,128)}) async-done(((f32[16,16384]{1,0:T(8,128)}, f32[16,3,16384]{2,0,1:T(8,128)}), (f32[16,16384]{1,0:T(8,128)}, f32[16,3,16384]{2,0,1:T(8,128)})) %all-reduce.5.cloned.1.call-update) | async-done | bytes 4194320
  332.6 1.8 dynamic-slice_bitcast_fusion.1
  334.5 1.9 collective-permute-start.2
  336.4 2.4 collective-permute-start.3
  338.8 2.3 constant_dynamic-slice_fusion
  341.1 0.0 collective-permute-done.2
  341.1 0.9 collective-permute-done.3
  342.0 2.3 fusion.18
  (7 shorter events, 0.1 us)
Async XLA Ops:
  7.2 123.4 %all-gather.2.cloned.1.call-start = ((), (), s32[]{:S(2)}) async-start(), calls=%async_computation | async-start | bytes 1671168 | tf_op jit(solution)/shard_map/all_gather | solution.py:50
  7.2 53.7 %collective-permute-start = (bf16[128,128]{1,0:T(8,128)(2,1)}, bf16[128,128]{1,0:T(8,128)(2,1)S(1)}, u32[]{:S(2)}, u32[]{:S(2)}) collective-permute-start(bf16[128,128]{1,0:T(8,128)(2,1)} %param.6), channel_id=1, source_target_pairs={{0,16},{16,32},{32,48},{48,64},{64,80},{80,96},{96,112},{112,128},... | collective-permute-start | bytes 98312 | tf_op jit(solution)/shard_map/ppermute | solution.py:15
  9.1 51.8 %collective-permute-start.1 = (bf16[128,128]{1,0:T(8,128)(2,1)}, bf16[128,128]{1,0:T(8,128)(2,1)S(1)}, u32[]{:S(2)}, u32[]{:S(2)}) collective-permute-start(bf16[128,128]{1,0:T(8,128)(2,1)} %param.6), channel_id=1, source_target_pairs={{16,0},{32,16},{48,32},{64,48},{80,64},{96,80},{112,96},{128,112},... | collective-permute-start | bytes 98312 | tf_op jit(solution)/shard_map/ppermute | solution.py:17
  46.1 14.9 %copy-start = (bf16[128,128]{1,0:T(8,128)(2,1)S(1)}, bf16[128,128]{1,0:T(8,128)(2,1)}, u32[]{:S(2)}) copy-start(bf16[128,128]{1,0:T(8,128)(2,1)} %param.6) | copy-start | bytes 98308
  61.6 271.0 %all-reduce.5.cloned.1.call-start = ((), (), s32[]{:S(2)}) async-start(), calls=%async_computation.1 | async-start | bytes 8388608
  104.8 13.8 %copy-start.1 = (s32[192]{0:T(256)S(1)}, s32[192]{0:T(256)}, u32[]{:S(2)}) copy-start(s32[192]{0:T(256)} %param.10) | copy-start | bytes 2308
  199.4 18.6 %copy-start.2 = (u32[256]{0:T(256)S(1)}, u32[256]{0:T(256)}, u32[]{:S(2)}) copy-start(u32[256]{0:T(256)} %constant.91) | copy-start | bytes 3076
  334.5 6.6 %collective-permute-start.2 = (f32[1,16384]{1,0:T(1,128)S(1)}, f32[1,16384]{1,0:T(1,128)S(1)}, u32[]{:S(2)}, u32[]{:S(2)}) collective-permute-start(f32[1,16384]{1,0:T(1,128)S(1)} %get-tuple-element.10), channel_id=1, source_target_pairs={{16,0},{32,16},{48,32},{64,48},{80,64},{96,80},{112,96},{128,112},... | collective-permute-start | bytes 196616 | tf_op jit(solution)/shard_map/ppermute | solution.py:27
  336.4 5.6 %collective-permute-start.3 = (f32[1,16384]{1,0:T(1,128)S(1)}, f32[1,16384]{1,0:T(1,128)S(1)}, u32[]{:S(2)}, u32[]{:S(2)}) collective-permute-start(f32[1,16384]{1,0:T(1,128)S(1)} %get-tuple-element.11), channel_id=1, source_target_pairs={{0,16},{16,32},{32,48},{48,64},{64,80},{80,96},{96,112},{112,128},... | collective-permute-start | bytes 196616 | tf_op jit(solution)/shard_map/ppermute | solution.py:27
Sparse Core Ops, SparseCore 0:
  61.8 49.4 all-gather.1
  218.1 114.4 all-reduce.4
where the time goes:
time: 355 us; the launch traced here: 351 us
  waiting for transfers between devices  115 us (32%)
  other arithmetic  64.5 us (18%)
  local copies, waits for them, and re-layouts  61.3 us (17%)
  matrix products  61 us (17%)
  blocking collectives  24.5 us (7%)
  between operations  14.8 us (4%)
  starting transfers between devices  9.97 us (3%)
    unnamed x3, waiting for transfers between devices  114 us
    concatenate x2, local copies, waits for them, and re-layouts, complex_join(): return jnp.concatenate([real_part, imag_part], axis=-1)  25.2 us
    all_gather x1, blocking collectives, local(): lax.all_gather(adjoint_weights, 'clu', axis=0, tiled=True)  24.5 us
    concatenate x2, other arithmetic, complex_join(): return jnp.concatenate([real_part, imag_part], axis=-1)  22.6 us
    sub x2, other arithmetic, complex_join(): real_part = prod[:, 0, :, :half] - prod[:, 1, :, half:]  19.1 us
    add x2, other arithmetic, complex_join(): imag_part = prod[:, 0, :, half:] + prod[:, 1, :, :half]  19 us
    dot_general x1, matrix products, local(): jnp.dot(chosen, forward, precision=lax.Precision.HIGHEST, preferred_eleme...  18.6 us
    dot_general x1, matrix products, local(): jnp.einsum('nkpq,nqc->nkpc', kernels, picked, preferred_element_type=jnp....  16.4 us
  transfers between devices with their start and end apart: 6, of which 2 were waited for; matrix products, arithmetic and copies ran while one was open for 27% of the time, Pallas kernels for 0%

commit v1 on v0

v1 whole, which is shorter than its diff:
```python
import functools

import jax
import jax.numpy as jnp
from jax import lax
from jax.experimental import pallas as pl
from jax.experimental.pallas import tpu as pltpu
from jax.sharding import PartitionSpec as P

MESH = pl.DeviceIdType.MESH
SIDE = 4
UNROLL = 8
REL = (2, 1, 3, 0)


class Links:
    def __init__(self, send, recv):
        self.send_sem, self.recv_sem, self.open = send, recv, []

    def make(self, index, src, dst, device):
        return pltpu.make_async_remote_copy(
            src_ref=src,
            dst_ref=dst,
            send_sem=self.send_sem.at[index],
            recv_sem=self.recv_sem.at[index],
            device_id=device,
            device_id_type=MESH,
        )

    def start(self, index, src, dst, device, when=None):
        copy = self.make(index, src, dst, device)
        if when is None:
            copy.start()
        else:
            pl.when(when)(copy.start)
        self.open.append((copy, when))

    def arrived(self, index, dst, device):
        self.make(index, dst, dst, device).wait_recv()

    def finish(self):
        for copy, when in self.open:
            if when is None:
                copy.wait_send()
            else:
                pl.when(when)(copy.wait_send)


def kernel(
    groups,
    s_ref,
    w_ref,
    tab_ref,
    k_hbm,
    pot_ref,
    adj_ref,
    kbuf,
    run_buf,
    s_all,
    s_two,
    w_all,
    w_two,
    padj,
    ppot,
    zin,
    relay_in,
    relay_out,
    line_in,
    line_sum,
    half_in,
    half_out,
    last_in,
    ksem,
    send_sem,
    recv_sem,
):
    slots, _, panels, width = k_hbm.shape
    clu = w_all.shape[0]
    half = panels // 2
    cols = width // 2
    g = lax.axis_index("grp")
    c = lax.axis_index("clu")
    y, x = c // SIDE, c % SIDE
    has_up, has_down = g < groups - 1, g > 0
    up = {"grp": jnp.minimum(g + 1, groups - 1), "clu": c}
    down = {"grp": jnp.maximum(g - 1, 0), "clu": c}

    def at(a, p, q):
        return q * SIDE + p if a == "x" else p * SIDE + q

    place = {"x": (x, y), "y": (y, x)}

    def near(a, step):
        p, q = place[a]
        return {"grp": g, "clu": at(a, (p + step) % SIDE, q)}

    parts = ksem.shape[0]
    share = slots // parts
    kcopies = [
        pltpu.make_async_copy(
            k_hbm.at[pl.ds(i * share, share)], kbuf.at[pl.ds(i * share, share)], ksem.at[i]
        )
        for i in range(parts)
    ]
    for copy in kcopies:
        copy.start()
    w_all[c] = jnp.transpose(w_ref[...].astype(jnp.float32)).astype(jnp.bfloat16)
    s_all[clu + c] = s_ref[...]

    barrier = pltpu.get_barrier_semaphore()
    for a in ("x", "y"):
        for step in (1, 3):
            pl.semaphore_signal(barrier, inc=1, device_id=near(a, step), device_id_type=MESH)

    @pl.when(has_up)
    def _():
        pl.semaphore_signal(barrier, inc=1, device_id=up, device_id_type=MESH)

    @pl.when(has_down)
    def _():
        pl.semaphore_signal(barrier, inc=1, device_id=down, device_id_type=MESH)

    pl.semaphore_wait(barrier, 4 + has_up.astype(jnp.int32) + has_down.astype(jnp.int32))

    links = Links(send_sem, recv_sem)
    h0, h1 = pl.ds(0, half), pl.ds(half, half)

    W0, S0, ZS = 0, 20, 40
    sides = ((0, 1, h0), (1, 3, h1))

    def w_at(b):
        return w_all.at[b]

    def s_at(b):
        return s_all.at[clu + b]

    def to_groups(b, place_index):
        links.start(ZS + place_index, s_at(b), s_all.at[b], up, has_up)
        links.start(ZS + 16 + place_index, s_at(b), s_all.at[2 * clu + b], down, has_down)

    flows = (("x", "y", w_at, W0), ("y", "x", s_at, S0))

    def second(a1, a2, ref, base, slot, b):
        for d, step, _ in sides:
            links.start(base + 4 + d * 4 + slot, ref(b), ref(b), near(a2, step))

    for a1, a2, ref, base in flows:
        for d, step, _ in sides:
            links.start(base + d, ref(c), ref(c), near(a1, step))
    for a1, a2, ref, base in flows:
        second(a1, a2, ref, base, 0, c)
    to_groups(c, 0)
    for d, step, part in sides:
        for a1, a2, ref, base in flows:
            p, q = place[a1]
            b = at(a1, (p - step) % SIDE, q)
            links.arrived(base + d, ref(b), near(a1, step))
            links.start(base + 2 + d, ref(b).at[part], ref(b).at[part], near(a1, step))
            second(a1, a2, ref, base, 1 + d, b)
            if a1 == "y":
                to_groups(b, 1 + d)
    for a1, a2, ref, base in flows:
        p, q = place[a1]
        b = at(a1, (p + 2) % SIDE, q)
        for d, step, part in sides:
            links.arrived(base + 2 + d, ref(b).at[part], near(a1, step))
        second(a1, a2, ref, base, 3, b)
        if a1 == "y":
            to_groups(b, 3)
    order = (0, 3, 1, 2)
    for slot in range(4):
        for d, step, part in sides:
            for a1, a2, ref, base in flows:
                p, q = place[a1]
                b = at(a1, (p + order[slot]) % SIDE, (q - step) % SIDE)
                links.arrived(base + 4 + d * 4 + slot, ref(b), near(a2, step))
                links.start(base + 12 + d * 4 + slot, ref(b).at[part], ref(b).at[part], near(a2, step))
                if a1 == "y":
                    to_groups(b, 4 + slot * 2 + d)
    for slot in range(4):
        for a1, a2, ref, base in flows:
            p, q = place[a1]
            b = at(a1, (p + order[slot]) % SIDE, (q + 2) % SIDE)
            for d, step, part in sides:
                links.arrived(base + 12 + d * 4 + slot, ref(b).at[part], near(a2, step))
            if a1 == "y":
                to_groups(b, 12 + slot)

    def widen_w(t, carry):
        block = w_all[t]
        w_two[t, :, pl.ds(0, panels)] = block
        w_two[t, :, pl.ds(panels, panels)] = jnp.concatenate([-block[cols:], block[:cols]], axis=0)
        return carry

    lax.fori_loop(0, clu, widen_w, 0)
    for copy in kcopies:
        copy.wait()

    def sums(row, product):
        def body(i, carry):
            total, last = carry
            for u in range(UNROLL):
                k = i * UNROLL + u
                code = tab_ref[row, k]
                mine = code >> 16
                keep = (mine == last).astype(jnp.float32)
                total = total * keep + product(code & 255, (code >> 8) & 255)
                run_buf[k] = total
                last = mine
            return total, last

        lax.fori_loop(
            0, slots // UNROLL, body, (jnp.zeros((panels, width), jnp.float32), jnp.int32(-1))
        )

    def pick(row, out, count):
        def body(b, carry):
            end = tab_ref[row, slots + b]
            begin = tab_ref[row, slots + jnp.maximum(b - 1, 0)] * (b > 0).astype(jnp.int32)
            some = (end > begin).astype(jnp.float32)
            out[b] = run_buf[jnp.maximum(end - 1, 0)] * some
            return carry

        lax.fori_loop(0, count, body, 0)

    def adjoint_product(n, t):
        return jnp.dot(
            w_two[t], kbuf[n].reshape(2 * panels, panels), preferred_element_type=jnp.float32
        )

    sums(1, adjoint_product)
    pick(1, padj, 3 * clu)

    ZA = 72
    ay, aq = place["y"]
    zorder = [at("y", (ay + i) % SIDE, (aq + REL[j]) % SIDE) for i in REL for j in range(4)]
    for i, b in enumerate(zorder):
        links.start(ZA + i, padj.at[2 * clu + b], zin.at[0, b], up, has_up)
        links.start(ZA + 16 + i, padj.at[b], zin.at[1, b], down, has_down)

    gorder = [c]
    yp, yq = place["y"]
    gorder += [at("y", (yp - 1) % SIDE, yq), at("y", (yp + 1) % SIDE, yq), at("y", (yp + 2) % SIDE, yq)]
    for slot in range(4):
        for _, step, _ in sides:
            gorder.append(at("y", (yp + order[slot]) % SIDE, (yq - step) % SIDE))
    for slot in range(4):
        gorder.append(at("y", (yp + order[slot]) % SIDE, (yq + 2) % SIDE))

    lane = lax.broadcasted_iota(jnp.int32, (panels, width), 1)
    sign = jnp.where(lane < cols, -1.0, 1.0).astype(jnp.float32)

    def widen_s(b, carry):
        block = s_all[b]
        s_two[b, pl.ds(0, panels)] = block
        turned = pltpu.roll(block.astype(jnp.float32), cols, 1) * sign
        s_two[b, pl.ds(panels, panels)] = turned.astype(jnp.bfloat16)
        return carry

    def no_s(b, carry):
        s_two[b] = jnp.zeros((2 * panels, width), jnp.bfloat16)
        return carry

    lax.fori_loop(clu, 2 * clu, widen_s, 0)

    @pl.when(has_down)
    def _():
        for i, b in enumerate(gorder):
            links.arrived(ZS + i, s_all.at[b], down)
        lax.fori_loop(0, clu, widen_s, 0)

    @pl.when(jnp.logical_not(has_down))
    def _():
        lax.fori_loop(0, clu, no_s, 0)

    @pl.when(has_up)
    def _():
        for i, b in enumerate(gorder):
            links.arrived(ZS + 16 + i, s_all.at[2 * clu + b], up)
        lax.fori_loop(2 * clu, 3 * clu, widen_s, 0)

    @pl.when(jnp.logical_not(has_up))
    def _():
        lax.fori_loop(2 * clu, 3 * clu, no_s, 0)

    def forward_product(n, s):
        block = kbuf[n]
        return jnp.dot(
            jnp.concatenate([block[0], block[1]], axis=1), s_two[s], preferred_element_type=jnp.float32
        )

    sums(0, forward_product)
    pick(0, ppot, clu)

    class Plane:
        def __init__(self, which, a1, a2, ref):
            self.w, self.a1, self.a2, self.ref = which, a1, a2, ref
            self.base = 104 + 18 * which
            self.p, self.q = place[a1]

        def block(self, dp, j):
            return self.ref(at(self.a1, (self.p + dp) % SIDE, (self.q + REL[j]) % SIDE))

        def first(self):
            w = self.w
            for j in range(4):
                d = j % 2
                links.start(
                    self.base + j, self.block(2, j), relay_in.at[w, j], near(self.a1, 1 if d == 0 else 3)
                )
            for j in range(4):
                d = 1 - j % 2
                links.start(
                    self.base + 4 + 4 * d + j,
                    self.block(1 if d == 0 else 3, j),
                    line_in.at[w, d, j],
                    near(self.a1, 1 if d == 0 else 3),
                )

        def relay(self):
            w = self.w
            for j in range(4):
                d = j % 2
                step = 1 if d == 0 else 3
                links.arrived(self.base + j, relay_in.at[w, j], near(self.a1, step))
                relay_out[w, j] = self.block(step, j)[...] + relay_in[w, j]
                links.start(
                    self.base + 4 + 4 * d + j, relay_out.at[w, j], line_in.at[w, d, j], near(self.a1, step)
                )

        def total(self):
            w = self.w
            for j in range(4):
                for d in range(2):
                    links.arrived(
                        self.base + 4 + 4 * d + j, line_in.at[w, d, j], near(self.a1, 1 if d == 0 else 3)
                    )
                line_sum[w, j] = self.block(0, j)[...] + line_in[w, 0, j] + line_in[w, 1, j]
                if j == 0:
                    for d, step, part in sides:
                        links.start(
                            self.base + 12 + d, line_sum.at[w, 0, part], half_in.at[w, d], near(self.a2, step)
                        )
                if j == 1:
                    links.start(
                        self.base + 15, line_sum.at[w, 1, h1], last_in.at[w, 0, h1], near(self.a2, 1)
                    )
                if j == 2:
                    links.start(
                        self.base + 16, line_sum.at[w, 2, h0], last_in.at[w, 1, h0], near(self.a2, 3)
                    )

        def relay_last(self):
            w = self.w
            for d, step, part in sides:
                links.arrived(self.base + 12 + d, half_in.at[w, d], near(self.a2, step))
                half_out[w, d] = line_sum[w, 1 + d, part] + half_in[w, d]
                links.start(
                    self.base + (14 if d == 0 else 17),
                    half_out.at[w, d],
                    last_in.at[w, d, part],
                    near(self.a2, step),
                )

        def last(self):
            w = self.w
            for d, step, _ in sides:
                for e, part in ((0, h0), (1, h1)):
                    links.arrived(
                        self.base + 14 + 2 * d + e, last_in.at[w, d, part], near(self.a2, step)
                    )
            return line_sum[w, 3] + last_in[w, 0] + last_in[w, 1]

    pot = Plane(0, "x", "y", lambda b: ppot.at[b])
    adj = Plane(1, "y", "x", lambda b: padj.at[clu + b])
    pot.first()
    pot.relay()
    for i, b in enumerate(zorder):

        @pl.when(has_down)
        def _(i=i, b=b):
            links.arrived(ZA + i, zin.at[0, b], down)
            padj[clu + b] += zin[0, b]

        @pl.when(has_up)
        def _(i=i, b=b):
            links.arrived(ZA + 16 + i, zin.at[1, b], up)
            padj[clu + b] += zin[1, b]

    adj.first()
    pot.total()
    adj.relay()
    pot.relay_last()
    adj.total()
    pot_ref[...] = pot.last()
    adj.relay_last()
    adj_ref[...] = jnp.transpose(adj.last())
    links.finish()


def local(groups, strengths, adjoint_weights, kernels, target_ids, source_ids, live_slots):
    slots, _, panels, _ = kernels.shape
    width = strengths.shape[1]
    clu = lax.axis_size("clu")
    g = lax.axis_index("grp")
    n = jnp.arange(slots, dtype=jnp.int32)
    live = n < live_slots[0]
    target = target_ids - g * clu
    source = source_ids - (g - 1) * clu
    place = jnp.stack([jnp.where(live, target, 3 * clu), jnp.where(live, source, 3 * clu)])
    key = place * 256 + n
    rank = jnp.sum((key[:, None, :] < key[:, :, None]).astype(jnp.int32), axis=2)
    load = place * 65536 + jnp.stack([source, target]) * 256 + n
    hit = rank[:, :, None] == n[None, None, :]
    codes = jnp.sum(jnp.where(hit, load[:, :, None], 0), axis=1)
    bound = (jnp.arange(3 * clu, dtype=jnp.int32) + 1) * 256
    ends = jnp.sum((key[:, None, :] < bound[None, :, None]).astype(jnp.int32), axis=2)
    table = jnp.concatenate([codes, ends], axis=1)
    f32, bf16 = jnp.float32, jnp.bfloat16
    vmem = pl.BlockSpec(memory_space=pltpu.VMEM)
    block = (panels, width)
    copies = 140
    return pl.pallas_call(
        functools.partial(kernel, groups),
        out_shape=(jax.ShapeDtypeStruct(block, f32), jax.ShapeDtypeStruct(block, f32)),
        in_specs=[
            vmem,
            vmem,
            pl.BlockSpec(memory_space=pltpu.SMEM),
            pl.BlockSpec(memory_space=pl.ANY),
        ],
        out_specs=(vmem, vmem),
        scratch_shapes=[
            pltpu.VMEM(kernels.shape, bf16),
            pltpu.VMEM((slots, *block), f32),
            pltpu.VMEM((3 * clu, *block), bf16),
            pltpu.VMEM((3 * clu, 2 * panels, width), bf16),
            pltpu.VMEM((clu, width, panels), bf16),
            pltpu.VMEM((clu, width, 2 * panels), bf16),
            pltpu.VMEM((3 * clu, *block), f32),
            pltpu.VMEM((clu, *block), f32),
            pltpu.VMEM((2, clu, *block), f32),
            pltpu.VMEM((2, 4, *block), f32),
            pltpu.VMEM((2, 4, *block), f32),
            pltpu.VMEM((2, 2, 4, *block), f32),
            pltpu.VMEM((2, 4, *block), f32),
            pltpu.VMEM((2, 2, panels // 2, width), f32),
            pltpu.VMEM((2, 2, panels // 2, width), f32),
            pltpu.VMEM((2, 2, *block), f32),
            pltpu.SemaphoreType.DMA((4,)),
            pltpu.SemaphoreType.DMA((copies,)),
            pltpu.SemaphoreType.DMA((copies,)),
        ],
        compiler_params=pltpu.CompilerParams(
            collective_id=0, has_side_effects=True, vmem_limit_bytes=60 * 1024 * 1024
        ),
    )(strengths, adjoint_weights, table, kernels)


def solution(mesh):
    spec = P(("grp", "clu"))
    rows = P(("grp", "clu"), None)
    return jax.shard_map(
        functools.partial(local, mesh.shape["grp"]),
        mesh=mesh,
        in_specs=(rows, rows, P(("grp", "clu"), None, None, None), spec, spec, spec),
        out_specs=(rows, rows),
        check_vma=False,
    )
```

time: 355 us -> 71.7 us (0.20); the launches traced: 351 us -> 71.4 us
  waiting for transfers between devices: 115 us -> 0 us
  Pallas kernels: 0 us -> 65.2 us
  other arithmetic: 64.5 us -> 2 us
  matrix products: 61 us -> 0 us
  local copies, waits for them, and re-layouts: 61.3 us -> 2.95 us
  blocking collectives: 24.5 us -> 0 us
  between operations: 14.8 us -> 1.3 us
  starting transfers between devices: 9.97 us -> 0 us
    unnamed x3 -> x0, waiting for transfers between devices: 114 us -> none
    pallas_call x0 -> x1, Pallas kernels: none -> 65.2 us  [local(): pl.pallas_call(functools.partial(kernel, groups), out_shape=(jax.ShapeDty...]
    dot_general x4 -> x0, matrix products: 61 us -> none  [the longest x1 18.6 us: local(): jnp.dot(chosen, forward, precision=lax.Precision.HIGHEST, preferred_eleme...]
    concatenate x2 -> x0, local copies, waits for them, and re-layouts: 25.2 us -> none  [complex_join(): return jnp.concatenate([real_part, imag_part], axis=-1)]
    all_gather x1 -> x0, blocking collectives: 24.5 us -> none  [local(): lax.all_gather(adjoint_weights, 'clu', axis=0, tiled=True)]
    concatenate x3 -> x1, other arithmetic: 23.3 us -> 0.65 us  [local(): table = jnp.concatenate([codes, ends], axis=1)]
    add x3 -> x1, other arithmetic: 21.3 us -> 0.01 us  [local(): load = place * 65536 + jnp.stack([source, target]) * 256 + n]
    sub x2 -> x0, other arithmetic: 19.1 us -> none  [complex_join(): real_part = prod[:, 0, :, :half] - prod[:, 1, :, half:]]
  transfers between devices with their start and end apart: 6 -> 0, of which waited for: 2 -> 0; matrix products, arithmetic and copies ran while one was open for 27% -> 0% of each run, Pallas kernels for 0% -> 0%
where the time goes in v1:
time: 71.7 us; the launch traced here: 71.4 us
  Pallas kernels  65.2 us (91%)
  local copies, waits for them, and re-layouts  2.95 us (4%)
  other arithmetic  2 us (3%)
  between operations  1.3 us (2%)
    pallas_call x1, Pallas kernels, local(): pl.pallas_call(functools.partial(kernel, groups), out_shape=(jax.ShapeDty...  65.2 us
    unnamed x2, local copies, waits for them, and re-layouts  2.95 us

profile of v1, /device:TPU:96, one launch (start us, length us, event | category | flops | bytes accessed | tf_op | source)
XLA Modules:
  0.0 71.4 jit_solution(17133300496376320936)
XLA Ops:
  1.3 0.7 fusion.2
  2.0 0.2 convert_reduce_fusion.1
  2.2 0.3 convert_reduce_fusion
  2.4 0.2 select_reduce_fusion
  2.6 0.7 pad_add_fusion.1.tab_ref
  3.3 65.2 %shard_map.77 = (f32[128,128]{1,0:T(8,128)}, f32[128,128]{1,0:T(8,128)}) custom-call(bf16[128,128]{1,0:T(8,128)(2,1)} %s_ref.1, bf16[128,128]{1,0:T(8,128)(2,1)} %w_ref.1, s32[2,240]{1,0:T(2,128)} %pad_add_fusion.1.tab_ref, bf16[192,2,128,128]{3,2,1,0:T(8,128)(2,1)} %k_hbm.1), custom_call_target="tpu_custom_call" | custom-call | tf_op jit(solution)/shard_map/pallas_call | solution.py:423
  68.5 1.5 %copy.11 = f32[128,128]{1,0:T(8,128)} copy(f32[128,128]{1,0:T(8,128)} %get-tuple-element.12) | data formatting | bytes 131072
  70.0 1.5 %copy.12 = f32[128,128]{1,0:T(8,128)} copy(f32[128,128]{1,0:T(8,128)} %get-tuple-element.13) | data formatting | bytes 131072
  (2 shorter events, 0.0 us)

commit v2 on v1

v2 whole, which is shorter than its diff:
```python
import functools

import jax
import jax.numpy as jnp
from jax import lax
from jax.experimental import pallas as pl
from jax.experimental.pallas import tpu as pltpu
from jax.sharding import PartitionSpec as P

MESH = pl.DeviceIdType.MESH
SIDE = 4
UNROLL = 16
REL = (2, 1, 3, 0)


class Links:
    def __init__(self, send, recv):
        self.send_sem, self.recv_sem, self.open = send, recv, []

    def make(self, index, src, dst, device):
        return pltpu.make_async_remote_copy(
            src_ref=src,
            dst_ref=dst,
            send_sem=self.send_sem.at[index],
            recv_sem=self.recv_sem.at[index],
            device_id=device,
            device_id_type=MESH,
        )

    def start(self, index, src, dst, device, when=None):
        copy = self.make(index, src, dst, device)
        if when is None:
            copy.start()
        else:
            pl.when(when)(copy.start)
        self.open.append((copy, when))

    def pool(self, index, src, dst, device, when):
        pl.when(when)(self.make(index, src, dst, device).start)

    def done(self, index, src, device, when):
        pl.when(when)(self.make(index, src, src, device).wait_send)

    def arrived(self, index, dst, device):
        self.make(index, dst, dst, device).wait_recv()

    def finish(self):
        for copy, when in self.open:
            if when is None:
                copy.wait_send()
            else:
                pl.when(when)(copy.wait_send)


def kernel(
    groups,
    s_ref,
    w_ref,
    tab_ref,
    k_hbm,
    pot_ref,
    adj_ref,
    kbuf,
    run_buf,
    s_all,
    s_two,
    w_all,
    w_two,
    padj,
    ppot,
    zin,
    line_in,
    line_sum,
    last_in,
    ksem,
    send_sem,
    recv_sem,
):
    slots, _, panels, width = k_hbm.shape
    clu = w_all.shape[0]
    half = panels // 2
    cols = width // 2
    g = lax.axis_index("grp")
    c = lax.axis_index("clu")
    y, x = c // SIDE, c % SIDE
    has_up, has_down = g < groups - 1, g > 0
    up = {"grp": jnp.minimum(g + 1, groups - 1), "clu": c}
    down = {"grp": jnp.maximum(g - 1, 0), "clu": c}

    def at(a, p, q):
        return q * SIDE + p if a == "x" else p * SIDE + q

    place = {"x": (x, y), "y": (y, x)}

    def near(a, step):
        p, q = place[a]
        return {"grp": g, "clu": at(a, (p + step) % SIDE, q)}

    parts = ksem.shape[0]
    share = slots // parts
    kcopies = [
        pltpu.make_async_copy(
            k_hbm.at[pl.ds(i * share, share)], kbuf.at[pl.ds(i * share, share)], ksem.at[i]
        )
        for i in range(parts)
    ]
    for copy in kcopies:
        copy.start()
    w_all[c] = jnp.transpose(w_ref[...].astype(jnp.float32)).astype(jnp.bfloat16)
    s_all[clu + c] = s_ref[...]

    barrier = pltpu.get_barrier_semaphore()
    for a in ("x", "y"):
        for step in (1, 2, 3):
            pl.semaphore_signal(barrier, inc=1, device_id=near(a, step), device_id_type=MESH)

    @pl.when(has_up)
    def _():
        pl.semaphore_signal(barrier, inc=1, device_id=up, device_id_type=MESH)

    @pl.when(has_down)
    def _():
        pl.semaphore_signal(barrier, inc=1, device_id=down, device_id_type=MESH)

    pl.semaphore_wait(barrier, 6 + has_up.astype(jnp.int32) + has_down.astype(jnp.int32))

    links = Links(send_sem, recv_sem)
    h0, h1 = pl.ds(0, half), pl.ds(half, half)
    STEPS = (1, 3, 2)

    class Flow:
        def __init__(self, base, a1, a2, part, ref):
            self.base, self.a1, self.a2, self.part, self.ref = base, a1, a2, part, ref
            self.p, self.q = place[a1]

        def piece(self, dp, dq):
            return at(self.a1, (self.p - dp) % SIDE, (self.q - dq) % SIDE)

        def send(self, index, b, axis, step):
            ref = self.ref(b).at[self.part]
            links.start(self.base + index, ref, ref, near(axis, step))

        def wait(self, index, b, axis, step):
            links.arrived(self.base + index, self.ref(b).at[self.part], near(axis, step))

        def begin(self):
            for i, step in enumerate(STEPS):
                self.send(i, self.piece(0, 0), self.a1, step)

        def spread(self, i):
            if i < 3:
                self.wait(i, self.piece(STEPS[i], 0), self.a1, STEPS[i])
            b = self.piece(STEPS[i] if i < 3 else 0, 0)
            for j, step in enumerate(STEPS):
                self.send(3 + 3 * i + j, b, self.a2, step)
            return b

        def late(self, i, j):
            b = self.piece(STEPS[i] if i < 3 else 0, STEPS[j])
            self.wait(3 + 3 * i + j, b, self.a2, STEPS[j])
            return b

    def w_at(b):
        return w_all.at[b]

    def s_at(b):
        return s_all.at[clu + b]

    w_flows = (Flow(0, "x", "y", h0, w_at), Flow(15, "y", "x", h1, w_at))
    s_flows = (Flow(30, "y", "x", h0, s_at), Flow(45, "x", "y", h1, s_at))
    ZS = 60

    def to_groups(flow, b):
        part = flow.part
        links.pool(ZS, s_at(b).at[part], s_all.at[b, part], up, has_up)
        links.pool(ZS + 1, s_at(b).at[part], s_all.at[2 * clu + b, part], down, has_down)

    for flow in w_flows + s_flows:
        flow.begin()
    for flow in w_flows:
        flow.spread(3)
    for flow in s_flows:
        flow.spread(3)
        to_groups(flow, c)
    for i in range(3):
        for flow in w_flows:
            flow.spread(i)
        for flow in s_flows:
            to_groups(flow, flow.spread(i))
    order = [(i, j) for i in (3, 0, 1, 2) for j in range(3)]
    for i, j in order:
        for flow in w_flows:
            flow.late(i, j)

    def strengths_on(pairs):
        def hook():
            for i, j in pairs:
                for flow in s_flows:
                    to_groups(flow, flow.late(i, j))

        return hook

    def widen_w(t, carry):
        block = w_all[t]
        w_two[t, :, pl.ds(0, panels)] = block
        w_two[t, :, pl.ds(panels, panels)] = jnp.concatenate([-block[cols:], block[:cols]], axis=0)
        return carry

    lax.fori_loop(0, clu, widen_w, 0)
    for copy in kcopies:
        copy.wait()

    def sums(row, product, hooks):
        def body(i, carry):
            total, last = carry
            for u in range(UNROLL):
                k = i * UNROLL + u
                code = tab_ref[row, k]
                mine = code >> 16
                keep = (mine == last).astype(jnp.float32)
                total = total * keep + product(code & 255, (code >> 8) & 255)
                run_buf[k] = total
                last = mine
            return total, last

        trips = slots // UNROLL
        carry = (jnp.zeros((panels, width), jnp.float32), jnp.int32(-1))
        for n, hook in enumerate(hooks):
            carry = lax.fori_loop(
                trips * n // len(hooks), trips * (n + 1) // len(hooks), body, carry
            )
            if hook is not None:
                hook()

    def pick(row, out, begin, count):
        def body(b, carry):
            end = tab_ref[row, slots + b]
            start = tab_ref[row, slots + jnp.maximum(b - 1, 0)] * (b > 0).astype(jnp.int32)
            some = (end > start).astype(jnp.float32)
            out[b] = run_buf[jnp.maximum(end - 1, 0)] * some
            return carry

        lax.fori_loop(begin, begin + count, body, 0)

    def adjoint_product(n, t):
        return jnp.dot(
            w_two[t], kbuf[n].reshape(2 * panels, panels), preferred_element_type=jnp.float32
        )

    sums(1, adjoint_product, (strengths_on(order[:6]), strengths_on(order[6:]), None))

    ZA = 62
    offsets = sorted(
        ((dy, dx) for dy in range(SIDE) for dx in range(SIDE)),
        key=lambda o: (min(REL.index(o[0]), REL.index(o[1])), REL.index(o[0]) + REL.index(o[1])),
    )

    def block_at(o):
        return (y + o[0]) % SIDE * SIDE + (x + o[1]) % SIDE

    pick(1, padj, 2 * clu, clu)
    for i, o in enumerate(offsets):
        b = block_at(o)
        links.start(ZA + i, padj.at[2 * clu + b], zin.at[0, b], up, has_up)
    pick(1, padj, 0, clu)
    for i, o in enumerate(offsets):
        b = block_at(o)
        links.start(ZA + 16 + i, padj.at[b], zin.at[1, b], down, has_down)
    pick(1, padj, clu, clu)

    class Half:
        def __init__(self, which, side, a1, a2, part, ref):
            self.w, self.s, self.a1, self.a2, self.part, self.ref = which, side, a1, a2, part, ref
            self.base = 94 + 30 * which + 15 * side
            self.p, self.q = place[a1]

        def send(self, o):
            dp, dq = (o[1], o[0]) if self.a1 == "x" else o
            if dp == 0:
                return
            i, j = REL.index(dp), REL.index(dq)
            links.start(
                self.base + 4 * i + j,
                self.ref(block_at(o)).at[self.part],
                line_in.at[self.w, self.s, i, j],
                near(self.a1, dp),
            )

        def total(self, j):
            for i in range(3):
                links.arrived(
                    self.base + 4 * i + j, line_in.at[self.w, self.s, i, j], near(self.a1, REL[i])
                )
            b = at(self.a1, self.p, (self.q + REL[j]) % SIDE)
            got = line_in.at[self.w, self.s]
            line_sum[self.w, self.s, j] = self.ref(b)[self.part] + got[0, j] + got[1, j] + got[2, j]
            if j < 3:
                links.start(
                    self.base + 12 + j,
                    line_sum.at[self.w, self.s, j],
                    last_in.at[self.w, self.s, j],
                    near(self.a2, REL[j]),
                )

        def last(self):
            got = last_in.at[self.w, self.s]
            for j in range(3):
                links.arrived(self.base + 12 + j, got.at[j], near(self.a2, REL[j]))
            return line_sum[self.w, self.s, 3] + got[0] + got[1] + got[2]

    def halves(which, ref):
        return (
            Half(which, 0, "x", "y", h0, ref),
            Half(which, 1, "y", "x", h1, ref),
        )

    pots = halves(0, lambda b: ppot.at[b])
    adjs = halves(1, lambda b: padj.at[clu + b])

    def adjoint_on(low, high):
        def hook():
            for i in range(low, high):
                b = block_at(offsets[i])

                @pl.when(has_down)
                def _(i=i, b=b):
                    links.arrived(ZA + i, zin.at[0, b], down)
                    padj[clu + b] += zin[0, b]

                @pl.when(has_up)
                def _(i=i, b=b):
                    links.arrived(ZA + 16 + i, zin.at[1, b], up)
                    padj[clu + b] += zin[1, b]

                for part in adjs:
                    part.send(offsets[i])

        return hook

    lane = lax.broadcasted_iota(jnp.int32, (panels, width), 1)
    sign = jnp.where(lane < cols, -1.0, 1.0).astype(jnp.float32)

    def widen_s(b, carry):
        block = s_all[b]
        s_two[b, pl.ds(0, panels)] = block
        turned = pltpu.roll(block.astype(jnp.float32), cols, 1) * sign
        s_two[b, pl.ds(panels, panels)] = turned.astype(jnp.bfloat16)
        return carry

    def no_s(b, carry):
        s_two[b] = jnp.zeros((2 * panels, width), jnp.bfloat16)
        return carry

    lax.fori_loop(clu, 2 * clu, widen_s, 0)

    @pl.when(has_down)
    def _():
        links.arrived(ZS, s_all.at[pl.ds(0, clu)], down)
        lax.fori_loop(0, clu, widen_s, 0)

    @pl.when(jnp.logical_not(has_down))
    def _():
        lax.fori_loop(0, clu, no_s, 0)

    @pl.when(has_up)
    def _():
        links.arrived(ZS + 1, s_all.at[pl.ds(2 * clu, clu)], up)
        lax.fori_loop(2 * clu, 3 * clu, widen_s, 0)

    @pl.when(jnp.logical_not(has_up))
    def _():
        lax.fori_loop(2 * clu, 3 * clu, no_s, 0)

    def forward_product(n, s):
        block = kbuf[n]
        return jnp.dot(
            jnp.concatenate([block[0], block[1]], axis=1), s_two[s], preferred_element_type=jnp.float32
        )

    sums(0, forward_product, (None, None, adjoint_on(0, 4), None))
    pick(0, ppot, 0, clu)
    for o in offsets:
        for part in pots:
            part.send(o)
    adjoint_on(4, 16)()
    for group in (pots, adjs):
        for j in range(4):
            for part in group:
                part.total(j)
    for part in pots:
        pot_ref[part.part] = part.last()
    adj_ref[...] = jnp.transpose(jnp.concatenate([part.last() for part in adjs], axis=0))
    links.done(ZS, s_all.at[pl.ds(clu, clu)], up, has_up)
    links.done(ZS + 1, s_all.at[pl.ds(clu, clu)], down, has_down)
    links.finish()


def local(groups, strengths, adjoint_weights, kernels, target_ids, source_ids, live_slots):
    slots, _, panels, _ = kernels.shape
    width = strengths.shape[1]
    clu = lax.axis_size("clu")
    g = lax.axis_index("grp")
    n = jnp.arange(slots, dtype=jnp.int32)
    live = n < live_slots[0]
    target = target_ids - g * clu
    source = source_ids - (g - 1) * clu
    place = jnp.stack([jnp.where(live, target, 3 * clu), jnp.where(live, source, 3 * clu)])
    key = place * 256 + n
    rank = jnp.sum((key[:, None, :] < key[:, :, None]).astype(jnp.int32), axis=2)
    load = place * 65536 + jnp.stack([source, target]) * 256 + n
    hit = rank[:, :, None] == n[None, None, :]
    codes = jnp.sum(jnp.where(hit, load[:, :, None], 0), axis=1)
    bound = (jnp.arange(3 * clu, dtype=jnp.int32) + 1) * 256
    ends = jnp.sum((key[:, None, :] < bound[None, :, None]).astype(jnp.int32), axis=2)
    table = jnp.concatenate([codes, ends], axis=1)
    f32, bf16 = jnp.float32, jnp.bfloat16
    vmem = pl.BlockSpec(memory_space=pltpu.VMEM)
    block = (panels, width)
    copies = 154
    return pl.pallas_call(
        functools.partial(kernel, groups),
        out_shape=(jax.ShapeDtypeStruct(block, f32), jax.ShapeDtypeStruct(block, f32)),
        in_specs=[
            vmem,
            vmem,
            pl.BlockSpec(memory_space=pltpu.SMEM),
            pl.BlockSpec(memory_space=pl.ANY),
        ],
        out_specs=(vmem, vmem),
        scratch_shapes=[
            pltpu.VMEM(kernels.shape, bf16),
            pltpu.VMEM((slots, *block), f32),
            pltpu.VMEM((3 * clu, *block), bf16),
            pltpu.VMEM((3 * clu, 2 * panels, width), bf16),
            pltpu.VMEM((clu, width, panels), bf16),
            pltpu.VMEM((clu, width, 2 * panels), bf16),
            pltpu.VMEM((3 * clu, *block), f32),
            pltpu.VMEM((clu, *block), f32),
            pltpu.VMEM((2, clu, *block), f32),
            pltpu.VMEM((2, 2, 3, 4, panels // 2, width), f32),
            pltpu.VMEM((2, 2, 4, panels // 2, width), f32),
            pltpu.VMEM((2, 2, 3, panels // 2, width), f32),
            pltpu.SemaphoreType.DMA((4,)),
            pltpu.SemaphoreType.DMA((copies,)),
            pltpu.SemaphoreType.DMA((copies,)),
        ],
        compiler_params=pltpu.CompilerParams(
            collective_id=0, has_side_effects=True, vmem_limit_bytes=60 * 1024 * 1024
        ),
    )(strengths, adjoint_weights, table, kernels)


def solution(mesh):
    spec = P(("grp", "clu"))
    rows = P(("grp", "clu"), None)
    return jax.shard_map(
        functools.partial(local, mesh.shape["grp"]),
        mesh=mesh,
        in_specs=(rows, rows, P(("grp", "clu"), None, None, None), spec, spec, spec),
        out_specs=(rows, rows),
        check_vma=False,
    )
```

time: 71.7 us -> 57.1 us (0.80)
  Pallas kernels: 65.2 us -> 50.4 us
    pallas_call x1, Pallas kernels: 65.2 us -> 50.4 us  [local(): pl.pallas_call(functools.partial(kernel, groups), out_shape=(jax.ShapeDty...]
where the time goes in v2:
time: 57.1 us; the launch traced here: 56.6 us
  Pallas kernels  50.4 us (88%)
  local copies, waits for them, and re-layouts  2.95 us (5%)
  other arithmetic  2 us (4%)
  between operations  1.3 us (2%)
    pallas_call x1, Pallas kernels, local(): pl.pallas_call(functools.partial(kernel, groups), out_shape=(jax.ShapeDty...  50.4 us
    unnamed x2, local copies, waits for them, and re-layouts  2.95 us

profile of v2, /device:TPU:96, one launch (start us, length us, event | category | flops | bytes accessed | tf_op | source)
XLA Modules:
  0.0 56.6 jit_solution(3879092410966677035)
XLA Ops:
  1.3 0.7 %fusion.2 = (s32[192]{0:T(256)S(1)}, s32[192]{0:T(256)S(1)}, s32[192]{0:T(256)S(1)}, s32[192]{0:T(256)S(1)}) fusion(s32[]{:T(128)} %bitcast.5, s32[192]{0:T(256)} %param.10, s32[]{:T(128)S(6)} %mul.45, s32[192]{0:T(256)} %param.9, s32[]{:T(128)S(6)} %mul.44), kind=kLoop, calls=%fused_computation.11 | loop fusion | flops 960 | bytes 4620 | tf_op jit(solution)/shard_map/jit(_where)/select_n | solution.py:407
  2.0 0.2 convert_reduce_fusion.1
  2.2 0.3 convert_reduce_fusion
  2.4 0.2 select_reduce_fusion
  2.6 0.7 %pad_add_fusion.1.tab_ref = s32[2,240]{1,0:T(2,128)} fusion(s32[2,48]{1,0:T(2,128)S(1)} %convert_reduce_fusion.1, s32[2,192]{1,0:T(2,128)S(1)} %select_reduce_fusion), kind=kLoop, calls=%fused_computation.8 | loop fusion | flops 480 | bytes 3840 | tf_op jit(solution)/shard_map/concatenate | solution.py:415
  3.3 50.4 %shard_map.77 = (f32[128,128]{1,0:T(8,128)}, f32[128,128]{1,0:T(8,128)}) custom-call(bf16[128,128]{1,0:T(8,128)(2,1)} %s_ref.1, bf16[128,128]{1,0:T(8,128)(2,1)} %w_ref.1, s32[2,240]{1,0:T(2,128)} %pad_add_fusion.1.tab_ref, bf16[192,2,128,128]{3,2,1,0:T(8,128)(2,1)} %k_hbm.1), custom_call_target="tpu_custom_call" | custom-call | tf_op jit(solution)/shard_map/pallas_call | solution.py:420
  53.7 1.5 %copy.11 = f32[128,128]{1,0:T(8,128)} copy(f32[128,128]{1,0:T(8,128)} %get-tuple-element.12) | data formatting | bytes 131072
  55.2 1.5 %copy.12 = f32[128,128]{1,0:T(8,128)} copy(f32[128,128]{1,0:T(8,128)} %get-tuple-element.13) | data formatting | bytes 131072
  (2 shorter events, 0.0 us)

commit v3 on v2

--- a/solution.py
+++ b/solution.py
@@ -9,7 +9,7 @@
 
 MESH = pl.DeviceIdType.MESH
 SIDE = 4
-UNROLL = 16
+UNROLL = 32
 REL = (2, 1, 3, 0)
 
 
@@ -58,8 +58,7 @@
     w_ref,
     tab_ref,
     k_hbm,
-    pot_ref,
-    adj_ref,
+    out_ref,
     kbuf,
     run_buf,
     s_all,
@@ -388,8 +387,8 @@
             for part in group:
                 part.total(j)
     for part in pots:
-        pot_ref[part.part] = part.last()
-    adj_ref[...] = jnp.transpose(jnp.concatenate([part.last() for part in adjs], axis=0))
+        out_ref[0, part.part] = part.last()
+    out_ref[1] = jnp.transpose(jnp.concatenate([part.last() for part in adjs], axis=0))
     links.done(ZS, s_all.at[pl.ds(clu, clu)], up, has_up)
     links.done(ZS + 1, s_all.at[pl.ds(clu, clu)], down, has_down)
     links.finish()
@@ -417,16 +416,16 @@
     vmem = pl.BlockSpec(memory_space=pltpu.VMEM)
     block = (panels, width)
     copies = 154
-    return pl.pallas_call(
+    both = pl.pallas_call(
         functools.partial(kernel, groups),
-        out_shape=(jax.ShapeDtypeStruct(block, f32), jax.ShapeDtypeStruct(block, f32)),
+        out_shape=pltpu.VMEM((2, *block), f32),
         in_specs=[
             vmem,
             vmem,
             pl.BlockSpec(memory_space=pltpu.SMEM),
             pl.BlockSpec(memory_space=pl.ANY),
         ],
-        out_specs=(vmem, vmem),
+        out_specs=vmem,
         scratch_shapes=[
             pltpu.VMEM(kernels.shape, bf16),
             pltpu.VMEM((slots, *block), f32),
@@ -448,6 +447,7 @@
             collective_id=0, has_side_effects=True, vmem_limit_bytes=60 * 1024 * 1024
         ),
     )(strengths, adjoint_weights, table, kernels)
+    return both[0], both[1]
 
 
 def solution(mesh):

time: 57.1 us -> 52.4 us (0.918)
  Pallas kernels: 50.4 us -> 47.9 us
  local copies, waits for them, and re-layouts: 2.95 us -> 0.66 us
    unnamed x2 -> x0, local copies, waits for them, and re-layouts: 2.95 us -> none
    pallas_call x1, Pallas kernels: 50.4 us -> 47.9 us  [local(): pl.pallas_call(functools.partial(kernel, groups), out_shape=pltpu.VMEM((2...]
    squeeze x0 -> x1, local copies, waits for them, and re-layouts: none -> 0.66 us  [local(): return (both[0], both[1])]
where the time goes in v3:
time: 52.4 us; the launch traced here: 51.8 us
  Pallas kernels  47.9 us (91%)
  other arithmetic  2 us (4%)
  between operations  1.3 us (2%)
  local copies, waits for them, and re-layouts  0.66 us (1%)
    pallas_call x1, Pallas kernels, local(): pl.pallas_call(functools.partial(kernel, groups), out_shape=pltpu.VMEM((2...  47.9 us

profile of v3, /device:TPU:96, one launch (start us, length us, event | category | flops | bytes accessed | tf_op | source)
XLA Modules:
  0.0 51.8 jit_solution(14643612374704333432)
XLA Ops:
  1.3 0.7 %fusion.2 = (s32[192]{0:T(256)S(1)}, s32[192]{0:T(256)S(1)}, s32[192]{0:T(256)S(1)}, s32[192]{0:T(256)S(1)}) fusion(s32[]{:T(128)} %bitcast.9, s32[192]{0:T(256)} %param.10, s32[]{:T(128)S(6)} %mul.45, s32[192]{0:T(256)} %param.9, s32[]{:T(128)S(6)} %mul.44), kind=kLoop, calls=%fused_computation.13 | loop fusion | flops 960 | bytes 4620 | tf_op jit(solution)/shard_map/jit(_where)/select_n | solution.py:406
  2.0 0.2 convert_reduce_fusion.1
  2.2 0.3 convert_reduce_fusion
  2.4 0.2 select_reduce_fusion
  2.6 0.7 %pad_add_fusion.1.tab_ref = s32[2,240]{1,0:T(2,128)} fusion(s32[2,48]{1,0:T(2,128)S(1)} %convert_reduce_fusion.1, s32[2,192]{1,0:T(2,128)S(1)} %select_reduce_fusion), kind=kLoop, calls=%fused_computation.10 | loop fusion | flops 480 | bytes 3840 | tf_op jit(solution)/shard_map/concatenate | solution.py:414
  3.3 47.9 %shard_map.77 = f32[2,128,128]{2,1,0:T(8,128)S(1)} custom-call(bf16[128,128]{1,0:T(8,128)(2,1)} %s_ref.1, bf16[128,128]{1,0:T(8,128)(2,1)} %w_ref.1, s32[2,240]{1,0:T(2,128)} %pad_add_fusion.1.tab_ref, bf16[192,2,128,128]{3,2,1,0:T(8,128)(2,1)} %k_hbm.1), custom_call_target="tpu_custom_call" | custom-call | tf_op jit(solution)/shard_map/pallas_call | solution.py:419
  51.2 0.7 %slice_bitcast_fusion = (f32[128,128]{1,0:T(8,128)}, f32[128,128]{1,0:T(8,128)}) fusion(f32[2,128,128]{2,1,0:T(8,128)S(1)} %shard_map.77), kind=kLoop, calls=%fused_computation.4 | loop fusion | bytes 262144 | tf_op jit(solution)/shard_map/squeeze | solution.py:450
  (2 shorter events, 0.0 us)

commit v4 on v3

--- a/solution.py
+++ b/solution.py
@@ -56,7 +56,8 @@
     groups,
     s_ref,
     w_ref,
-    tab_ref,
+    ids_ref,
+    live_ref,
     k_hbm,
     out_ref,
     kbuf,
@@ -71,6 +72,10 @@
     line_in,
     line_sum,
     last_in,
+    rows,
+    codes,
+    tab_ref,
+    tab_sem,
     ksem,
     send_sem,
     recv_sem,
@@ -95,6 +100,19 @@
         p, q = place[a]
         return {"grp": g, "clu": at(a, (p + step) % SIDE, q)}
 
+    barrier = pltpu.get_barrier_semaphore()
+    for a in ("x", "y"):
+        for step in (1, 2, 3):
+            pl.semaphore_signal(barrier, inc=1, device_id=near(a, step), device_id_type=MESH)
+
+    @pl.when(has_up)
+    def _():
+        pl.semaphore_signal(barrier, inc=1, device_id=up, device_id_type=MESH)
+
+    @pl.when(has_down)
+    def _():
+        pl.semaphore_signal(barrier, inc=1, device_id=down, device_id_type=MESH)
+
     parts = ksem.shape[0]
     share = slots // parts
     kcopies = [
@@ -108,24 +126,37 @@
     w_all[c] = jnp.transpose(w_ref[...].astype(jnp.float32)).astype(jnp.bfloat16)
     s_all[clu + c] = s_ref[...]
 
-    barrier = pltpu.get_barrier_semaphore()
-    for a in ("x", "y"):
-        for step in (1, 2, 3):
-            pl.semaphore_signal(barrier, inc=1, device_id=near(a, step), device_id_type=MESH)
-
-    @pl.when(has_up)
-    def _():
-        pl.semaphore_signal(barrier, inc=1, device_id=up, device_id_type=MESH)
-
-    @pl.when(has_down)
-    def _():
-        pl.semaphore_signal(barrier, inc=1, device_id=down, device_id_type=MESH)
-
-    pl.semaphore_wait(barrier, 6 + has_up.astype(jnp.int32) + has_down.astype(jnp.int32))
-
     links = Links(send_sem, recv_sem)
     h0, h1 = pl.ds(0, half), pl.ds(half, half)
     STEPS = (1, 3, 2)
+
+    def tables():
+        span = rows.shape[1]
+        number = lax.broadcasted_iota(jnp.int32, (1, span), 1)
+        live = number < live_ref[0]
+        rows[...] = jnp.zeros_like(rows)
+        rows[pl.ds(0, 2), pl.ds(0, slots)] = ids_ref[...]
+        across = lax.broadcasted_iota(jnp.int32, (span, span), 1)
+        down = lambda row: jnp.transpose(jnp.broadcast_to(row, (span, span)))
+        locals_ = [
+            jnp.clip(rows[pl.ds(0, 1)] - g * clu, 0, clu - 1),
+            jnp.clip(rows[pl.ds(1, 1)] - (g - 1) * clu, 0, 3 * clu - 1),
+        ]
+        for i in range(2):
+            spot = jnp.where(live, locals_[i], 3 * clu)
+            key = spot * 256 + number
+            key_down = down(key)
+            rank = jnp.sum((key_down < key).astype(jnp.int32), axis=0, keepdims=True)
+            load = down(spot * 65536 + locals_[1 - i] * 256 + number)
+            codes[pl.ds(i, 1)] = jnp.sum(jnp.where(down(rank) == across, load, 0), axis=0, keepdims=True)
+            ends = (key_down < (across + 1) * 256).astype(jnp.int32)
+            codes[pl.ds(2 + i, 1)] = jnp.sum(ends, axis=0, keepdims=True)
+        copy = pltpu.make_async_copy(codes, tab_ref, tab_sem)
+        copy.start()
+        return copy
+
+    table_copy = tables()
+    pl.semaphore_wait(barrier, 6 + has_up.astype(jnp.int32) + has_down.astype(jnp.int32))
 
     class Flow:
         def __init__(self, base, a1, a2, part, ref):
@@ -208,6 +239,7 @@
     lax.fori_loop(0, clu, widen_w, 0)
     for copy in kcopies:
         copy.wait()
+    table_copy.wait()
 
     def sums(row, product, hooks):
         def body(i, carry):
@@ -233,8 +265,8 @@
 
     def pick(row, out, begin, count):
         def body(b, carry):
-            end = tab_ref[row, slots + b]
-            start = tab_ref[row, slots + jnp.maximum(b - 1, 0)] * (b > 0).astype(jnp.int32)
+            end = tab_ref[2 + row, b]
+            start = tab_ref[2 + row, jnp.maximum(b - 1, 0)] * (b > 0).astype(jnp.int32)
             some = (end > start).astype(jnp.float32)
             out[b] = run_buf[jnp.maximum(end - 1, 0)] * some
             return carry
@@ -376,12 +408,16 @@
             jnp.concatenate([block[0], block[1]], axis=1), s_two[s], preferred_element_type=jnp.float32
         )
 
-    sums(0, forward_product, (None, None, adjoint_on(0, 4), None))
+    sums(
+        0,
+        forward_product,
+        (None, None, adjoint_on(0, 3), adjoint_on(3, 5), adjoint_on(5, 7), adjoint_on(7, 8)),
+    )
     pick(0, ppot, 0, clu)
     for o in offsets:
         for part in pots:
             part.send(o)
-    adjoint_on(4, 16)()
+    adjoint_on(8, 16)()
     for group in (pots, adjs):
         for j in range(4):
             for part in group:
@@ -398,20 +434,8 @@
     slots, _, panels, _ = kernels.shape
     width = strengths.shape[1]
     clu = lax.axis_size("clu")
-    g = lax.axis_index("grp")
-    n = jnp.arange(slots, dtype=jnp.int32)
-    live = n < live_slots[0]
-    target = target_ids - g * clu
-    source = source_ids - (g - 1) * clu
-    place = jnp.stack([jnp.where(live, target, 3 * clu), jnp.where(live, source, 3 * clu)])
-    key = place * 256 + n
-    rank = jnp.sum((key[:, None, :] < key[:, :, None]).astype(jnp.int32), axis=2)
-    load = place * 65536 + jnp.stack([source, target]) * 256 + n
-    hit = rank[:, :, None] == n[None, None, :]
-    codes = jnp.sum(jnp.where(hit, load[:, :, None], 0), axis=1)
-    bound = (jnp.arange(3 * clu, dtype=jnp.int32) + 1) * 256
-    ends = jnp.sum((key[:, None, :] < bound[None, :, None]).astype(jnp.int32), axis=2)
-    table = jnp.concatenate([codes, ends], axis=1)
+    ids = jnp.stack([target_ids, source_ids])
+    span = -(-slots // 128) * 128
     f32, bf16 = jnp.float32, jnp.bfloat16
     vmem = pl.BlockSpec(memory_space=pltpu.VMEM)
     block = (panels, width)
@@ -420,6 +444,7 @@
         functools.partial(kernel, groups),
         out_shape=pltpu.VMEM((2, *block), f32),
         in_specs=[
+            vmem,
             vmem,
             vmem,
             pl.BlockSpec(memory_space=pltpu.SMEM),
@@ -439,6 +464,10 @@
             pltpu.VMEM((2, 2, 3, 4, panels // 2, width), f32),
             pltpu.VMEM((2, 2, 4, panels // 2, width), f32),
             pltpu.VMEM((2, 2, 3, panels // 2, width), f32),
+            pltpu.VMEM((8, span), jnp.int32),
+            pltpu.VMEM((8, span), jnp.int32),
+            pltpu.SMEM((8, span), jnp.int32),
+            pltpu.SemaphoreType.DMA,
             pltpu.SemaphoreType.DMA((4,)),
             pltpu.SemaphoreType.DMA((copies,)),
             pltpu.SemaphoreType.DMA((copies,)),
@@ -446,7 +475,7 @@
         compiler_params=pltpu.CompilerParams(
             collective_id=0, has_side_effects=True, vmem_limit_bytes=60 * 1024 * 1024
         ),
-    )(strengths, adjoint_weights, table, kernels)
+    )(strengths, adjoint_weights, ids, live_slots, kernels)
     return both[0], both[1]
 
 

time: 52.4 us -> 50.5 us (0.964)
  Pallas kernels: 47.9 us -> 46.9 us
  other arithmetic: 2 us -> 1.28 us
    another operation x0 -> x1, other arithmetic: none -> 1.28 us  [local(): ids = jnp.stack([target_ids, source_ids])]
    pallas_call x1, Pallas kernels: 47.9 us -> 46.9 us  [local(): pl.pallas_call(functools.partial(kernel, groups), out_shape=pltpu.VMEM((2...]
    select_n x1 -> x0, other arithmetic: 0.7 us -> none  [local(): jnp.where(live, source, 3 * clu)]
    concatenate x1 -> x0, other arithmetic: 0.65 us -> none  [local(): table = jnp.concatenate([codes, ends], axis=1)]
    reduce_sum x3 -> x0, other arithmetic: 0.62 us -> none  [the longest x1 0.25 us: local(): jnp.sum((key[:, None, :] < key[:, :, None]).astype(jnp.int32), axis=2)]
where the time goes in v4:
time: 50.5 us; the launch traced here: 50.1 us
  Pallas kernels  46.9 us (93%)
  between operations  1.29 us (3%)
  other arithmetic  1.28 us (3%)
  local copies, waits for them, and re-layouts  0.66 us (1%)
    pallas_call x1, Pallas kernels, local(): pl.pallas_call(functools.partial(kernel, groups), out_shape=pltpu.VMEM((2...  46.9 us
    another operation x1, other arithmetic, local(): ids = jnp.stack([target_ids, source_ids])  1.28 us

profile of v4, /device:TPU:96, one launch (start us, length us, event | category | flops | bytes accessed | tf_op | source)
XLA Modules:
  0.0 50.1 jit_solution(12492624842565173021)
XLA Ops:
  1.3 1.3 %pad_add_fusion.ids_ref = s32[2,192]{1,0:T(2,128)} fusion(s32[1,192]{1,0:T(1,128)} %bitcast.6, s32[1,192]{1,0:T(1,128)} %bitcast.7), kind=kLoop, calls=%fused_computation.2 | loop fusion | flops 384 | bytes 3072 | tf_op jit(solution)/shard_map/stack | solution.py:437
  2.6 46.9 %shard_map.77 = f32[2,128,128]{2,1,0:T(8,128)S(1)} custom-call(bf16[128,128]{1,0:T(8,128)(2,1)} %s_ref.1, bf16[128,128]{1,0:T(8,128)(2,1)} %w_ref.1, s32[2,192]{1,0:T(2,128)} %pad_add_fusion.ids_ref, s32[1]{0:T(128)S(6)} %copy.8.live_ref, bf16[192,2,128,128]{3,2,1,0:T(8,128)(2,1)} %k_hbm.1), custom_call_target="tpu_custom_call" | custom-call | tf_op jit(solution)/shard_map/pallas_call | solution.py:443
  49.4 0.7 %slice_bitcast_fusion = (f32[128,128]{1,0:T(8,128)}, f32[128,128]{1,0:T(8,128)}) fusion(f32[2,128,128]{2,1,0:T(8,128)S(1)} %shard_map.77), kind=kLoop, calls=%fused_computation | loop fusion | bytes 262144 | tf_op jit(solution)/shard_map/squeeze | solution.py:479
